TPU v7x, 256 devices: a whole 4x4x8 slice. The times are simulated.
256 devices in a mesh: dp: 64 (over x, z, core), mp: 4 (over y).
Axes of the slice: x: 4, y: 4, z: 8, core: 2. Of those that a mesh axis runs over, the one named last changes fastest.
Arguments:
- history: bfloat16 [1024, 32, 1024], P('dp', None, 'mp'), may hold values from -6 to 6
- lengths: int32 [1024], replicated, may hold values from 1 to 32, 16384 in all
- source: int32 [1024], replicated, may hold values from 0 to 1023, as said below
- owners: int32 [32768, 8], P(('dp', 'mp')), may hold values from 0 to 255, all different within a row; in each aligned block of 128 rows (0 to 127, 128 to 255, ...) at most 6 rows name the same one
- item_rows: int32 [32768, 8], P(('dp', 'mp')), may hold values from 0 to 511
- catalogue: bfloat16 [131072, 1024], P(('dp', 'mp')), may hold values from -6 to 6
- w_in: bfloat16 [4, 1024, 1024], P(None, None, 'mp'), may hold values from -0.1875 to 0.1875
- w_out: bfloat16 [1024, 1024], P('mp'), may hold values from -0.1875 to 0.1875
Outputs:
- w_in_grad: float32 [4, 1024, 1024], P(None, 'dp', 'mp')
- w_out_grad: float32 [1024, 1024], P('mp', 'dp')
- cat_grad: float32 [131072, 1024], P(('dp', 'mp'))
Inputs may be any that keep to these rules, and one draw needn't show every extreme that they name: `source`: a permutation; balanced slot k lies on index k // 16 of dp, and the 16 histories that start on one index of dp go to one index of dp at most (16 + 64 - 1) // 64 at a time, that many for some index. Each event names 8 different owners, column 0 the positive item's; the events of one device (aligned blocks of 128) name one owner at most 6 times.
All inputs are finite; a program needn't handle non-finite values.
Results may differ from a plain program's by a relative error of at most 0.017.
Values may be sent and summed in bfloat16 or wider, within the bound.
A program may use at most 128 MiB of HBM per device.

v0:
```python
import jax
import jax.numpy as jnp
from jax import lax
from jax.sharding import PartitionSpec as P

DH = 128
cosine_divisor = 0.05
epsilon_norm = 1e-05
epsilon_unit = 1e-06


def normalize(rows_in):
    centered = rows_in - jnp.mean(rows_in, axis=-1, keepdims=True)
    spread = jnp.mean(centered * centered, axis=-1, keepdims=True)
    return centered / jnp.sqrt(spread + epsilon_norm)


def attend(projected, length_here):
    gating = projected[0]
    values = projected[1]
    queries = projected[2]
    key_rows = projected[3]
    steps_n = projected.shape[1]
    scores = jnp.einsum(
        "thd,shd->hts", queries, key_rows, preferred_element_type=jnp.float32
    ) / jnp.sqrt(jnp.float32(projected.shape[3]))
    places = jnp.arange(steps_n, dtype=jnp.int32)
    allowed = (places[None, :] <= places[:, None]) & (places[None, :] < length_here)
    weights = jnp.where(
        allowed[None], jax.nn.silu(scores) / length_here.astype(jnp.float32), 0.0
    ).astype(jnp.bfloat16)
    mixed_out = jnp.einsum("hts,shd->thd", weights, values, preferred_element_type=jnp.float32)
    return (normalize(mixed_out) * gating.astype(jnp.float32)).astype(jnp.bfloat16)


def loss_block(out_rows, valid_rows, fetched):
    out_norm = jnp.sqrt(jnp.sum(out_rows * out_rows, axis=-1, keepdims=True) + epsilon_unit)
    request_unit_vector = out_rows / out_norm
    item_f = fetched.astype(jnp.float32)
    item_norm = jnp.sqrt(jnp.sum(item_f * item_f, axis=-1, keepdims=True) + epsilon_unit)
    catalog_unit_vector = item_f / item_norm
    cosine_match_raw = (
        jnp.einsum("qn,qgn->qg", request_unit_vector, catalog_unit_vector) / cosine_divisor
    )
    expo = jnp.exp(cosine_match_raw)
    probs = expo / jnp.sum(expo, axis=-1, keepdims=True)
    column = jnp.arange(cosine_match_raw.shape[1], dtype=jnp.int32)
    exponent_shares = (probs - (column[None, :] == 0).astype(jnp.float32)) * valid_rows[
        :, None
    ].astype(jnp.float32)
    request_unit_vector_slope = (
        jnp.einsum("as,asy->ay", exponent_shares, catalog_unit_vector) / cosine_divisor
    )
    out_grad = (
        request_unit_vector_slope
        - request_unit_vector
        * jnp.sum(request_unit_vector * request_unit_vector_slope, axis=-1, keepdims=True)
    ) / out_norm
    catalog_unit_vector_slope = (
        exponent_shares[:, :, None] * request_unit_vector[:, None, :] / cosine_divisor
    )
    item_grad = (
        catalog_unit_vector_slope
        - catalog_unit_vector
        * jnp.sum(catalog_unit_vector * catalog_unit_vector_slope, axis=-1, keepdims=True)
    ) / item_norm
    return (out_grad, item_grad)


def silu_slope(preact):
    sigma = jax.nn.sigmoid(preact)
    return sigma * (1.0 + preact * (1.0 - sigma))


def earlier_same(labels):
    order_ids = jnp.arange(labels.shape[0], dtype=jnp.int32)
    same = (labels[None, :] == labels[:, None]) & (order_ids[None, :] < order_ids[:, None])
    return jnp.sum(same.astype(jnp.int32), axis=1)


def per_device(history, lengths, source, owners, item_rows, catalogue, w_in, w_out):
    dp_count = lax.axis_size("dp")
    mp_count = lax.axis_size("mp")
    dev_count = dp_count * mp_count
    here_dp = lax.axis_index("dp")
    here_mp = lax.axis_index("mp")
    seq_dev, steps_n, cols_here = history.shape
    seq_total = source.shape[0]
    per_peer = (seq_dev + dp_count - 1) // dp_count
    target = (
        jnp.zeros((seq_total,), jnp.int32).at[source].set(jnp.arange(seq_total, dtype=jnp.int32))
    )
    slot_ids = jnp.arange(seq_dev, dtype=jnp.int32)
    my_seqs = here_dp * seq_dev + slot_ids
    dest_dev = target[my_seqs] // seq_dev
    send_rank = earlier_same(dest_dev)
    outgoing = (
        jnp.zeros((dp_count, per_peer, steps_n, cols_here), jnp.bfloat16)
        .at[dest_dev, send_rank]
        .set(history)
    )
    arrived = lax.all_to_all(outgoing, "dp", split_axis=0, concat_axis=0, tiled=True)
    taken = source[my_seqs]
    anchor = taken // seq_dev
    anchor_block = anchor[:, None] * seq_dev + slot_ids[None, :]
    goes_here = target[anchor_block] // seq_dev == here_dp
    earlier = slot_ids[None, :] < (taken % seq_dev)[:, None]
    recv_rank = jnp.sum((goes_here & earlier).astype(jnp.int32), axis=1)
    counts = lengths[taken]
    local_rows = jnp.take(
        arrived.reshape(dp_count * per_peer, steps_n, cols_here),
        anchor * per_peer + recv_rank,
        axis=0,
    )
    features = lax.all_gather(local_rows, "mp", axis=2, tiled=True)
    rows_all = seq_dev * steps_n
    width = features.shape[2]
    flat_rows = features.reshape(rows_all, width)
    normed = normalize(flat_rows.astype(jnp.float32)).astype(jnp.bfloat16)
    preact = jnp.einsum("rd,cdh->crh", normed, w_in, preferred_element_type=jnp.float32)
    projected = jax.nn.silu(preact).astype(jnp.bfloat16)
    cols_heads = w_in.shape[2]
    heads_here = cols_heads // DH
    grouped = projected.reshape(4, seq_dev, steps_n, heads_here, DH)

    def run_all(inputs):
        return jax.vmap(attend, in_axes=(1, 0))(inputs, counts)

    gated, back = jax.vjp(run_all, grouped)
    gated_flat = gated.reshape(rows_all, cols_heads)
    partial_out = jnp.dot(gated_flat, w_out, preferred_element_type=jnp.float32)
    quarter = rows_all // mp_count
    summed = lax.psum(partial_out, "mp")
    out_rows = lax.dynamic_slice_in_dim(summed, here_mp * quarter, quarter, 0)
    out_rows = out_rows + lax.dynamic_slice_in_dim(flat_rows, here_mp * quarter, quarter, 0).astype(
        jnp.float32
    )
    position = here_mp * quarter + jnp.arange(quarter, dtype=jnp.int32)
    valid_rows = position % steps_n < counts[position // steps_n]
    top_n = owners.shape[1]
    asks = quarter * top_n
    capacity = max(2, (3 * asks + 2 * dev_count - 1) // (2 * dev_count))
    owner_flat = owners.reshape(-1)
    row_flat = item_rows.reshape(-1)
    rank_in = earlier_same(owner_flat)
    address = owner_flat * capacity + rank_in
    slot_table = (
        jnp.full((dev_count * capacity,), asks, jnp.int32)
        .at[address]
        .set(jnp.arange(asks, dtype=jnp.int32))
    )
    is_used = slot_table < asks
    safe_index = jnp.minimum(slot_table, asks - 1)
    wanted = jnp.where(is_used, row_flat[safe_index], 0).reshape(dp_count, mp_count, capacity)
    incoming = lax.all_to_all(
        lax.all_to_all(wanted, "dp", split_axis=0, concat_axis=0, tiled=True),
        "mp",
        split_axis=1,
        concat_axis=1,
        tiled=True,
    )
    incoming_flat = incoming.reshape(-1)
    looked = jnp.take(catalogue, incoming_flat, axis=0).reshape(dp_count, mp_count, capacity, width)
    returned = lax.all_to_all(
        lax.all_to_all(looked, "dp", split_axis=0, concat_axis=0, tiled=True),
        "mp",
        split_axis=1,
        concat_axis=1,
        tiled=True,
    )
    fetched = jnp.take(returned.reshape(dev_count * capacity, width), address, axis=0).reshape(
        quarter, top_n, width
    )
    out_grad, item_grad = loss_block(out_rows, valid_rows, fetched)
    item_flat = item_grad.reshape(asks, width)
    sending = jnp.where(is_used[:, None], jnp.take(item_flat, safe_index, axis=0), 0.0)
    landed = lax.all_to_all(
        lax.all_to_all(
            sending.reshape(dp_count, mp_count, capacity, width).astype(jnp.bfloat16),
            "dp",
            split_axis=0,
            concat_axis=0,
            tiled=True,
        ),
        "mp",
        split_axis=1,
        concat_axis=1,
        tiled=True,
    ).astype(jnp.float32)
    cat_grad = (
        jnp.zeros((catalogue.shape[0], width), jnp.float32)
        .at[incoming_flat]
        .add(landed.reshape(-1, width))
    )
    out_cotangent = lax.all_gather(out_grad.astype(jnp.bfloat16), "mp", axis=0, tiled=True)
    w_out_part = jnp.einsum(
        "rh,rd->hd", gated_flat, out_cotangent, preferred_element_type=jnp.float32
    )
    gated_cotangent = jnp.einsum(
        "rd,hd->rh", out_cotangent, w_out, preferred_element_type=jnp.float32
    ).astype(jnp.bfloat16)
    (grouped_cotangent,) = back(gated_cotangent.reshape(seq_dev, steps_n, heads_here, DH))
    projected_cotangent = grouped_cotangent.reshape(4, rows_all, cols_heads)
    preact_cotangent = (projected_cotangent.astype(jnp.float32) * silu_slope(preact)).astype(
        jnp.bfloat16
    )
    w_in_part = jnp.einsum(
        "rd,crh->cdh", normed, preact_cotangent, preferred_element_type=jnp.float32
    )
    w_in_grad, w_out_grad = (
        lax.psum_scatter(w_in_part, "dp", scatter_dimension=1, tiled=True),
        lax.psum_scatter(w_out_part, "dp", scatter_dimension=1, tiled=True),
    )
    return (w_in_grad, w_out_grad, cat_grad)


def solution(mesh):
    placed = (
        P("dp", None, "mp"),
        P(),
        P(),
        P(("dp", "mp"), None),
        P(("dp", "mp"), None),
        P(("dp", "mp"), None),
        P(None, None, "mp"),
        P("mp", None),
    )
    return jax.shard_map(
        per_device,
        mesh=mesh,
        in_specs=placed,
        out_specs=(P(None, "dp", "mp"), P("mp", "dp"), P(("dp", "mp"), None)),
        check_vma=False,
    )
```

profile of v0, /device:TPU:8, one launch (start us, length us, event | category | flops | bytes accessed | tf_op | source)
XLA Modules:
  0.0 688.2 jit_solution(856039338225278554)
XLA Ops:
  7.2 0.9 copy.110
  10.0 4.3 scatter_custom_fusion.2
  15.3 5.9 gather_fusion.5
  21.8 0.8 reshape.655
  22.6 11.9 %all-to-all-start.1 = ((s32[64,4,6]{2,1,0:T(4,128)}), s32[64,4,6]{2,1,0:T(4,128)S(1)}, u32[]{:S(2)}, u32[]{:S(2)}) async-start(s32[64,4,6]{2,1,0:T(4,128)} %reshape.655), calls=%async_computation.1 | async-start | bytes 262144 | tf_op jit(solution)/shard_map/all_to_all | solution.py:156
  35.3 4.3 scatter_custom_fusion
  40.4 4.4 all-to-all-done.1
  45.6 4.9 all-to-all-start.2
  50.6 1.1 broadcast.800
  51.7 2.7 scatter_fusion
  54.4 6.4 all-to-all-start
  62.7 5.8 gather_fusion.6
  68.6 6.2 gather.53
  74.8 2.6 broadcast_select_fusion
  77.4 7.9 %copy.116 = bf16[64,4,6,1024]{3,1,2,0:T(4,128)(2,1)} copy(bf16[64,4,6,1024]{3,2,1,0:T(8,128)(2,1)S(1)} %broadcast_select_fusion) | data formatting | bytes 6291456 | tf_op jit(solution)/shard_map/jit(_take)/select_n | solution.py:163
  85.2 3.5 all-to-all-done
  88.8 7.2 %all-to-all-start.3 = ((bf16[64,4,6,1024]{3,1,2,0:T(4,128)(2,1)}), bf16[64,4,6,1024]{3,1,2,0:T(4,128)(2,1)}, u32[]{:S(2)}, u32[]{:S(2)}) async-start(bf16[64,4,6,1024]{3,1,2,0:T(4,128)(2,1)} %copy.116), calls=%async_computation.3 | async-start | bytes 6291456 | tf_op jit(solution)/shard_map/all_to_all | solution.py:165
  96.0 1.4 gather_fusion.2
  97.7 1.8 gather_fusion.4
  101.8 27.1 %all-gather.3.cloned.1.call-done = bf16[16,32,1024]{2,1,0:T(8,128)(2,1)} async-done(((bf16[16,32,256]{2,1,0:T(8,128)(2,1)}), bf16[16,32,1024]{2,1,0:T(8,128)(2,1)}) %all-gather.3.cloned.1.call-update) | async-done | bytes 1048592 | tf_op jit(solution)/shard_map/all_gather | solution.py:115
  128.8 1.5 convert_reduce_fusion.1
  130.4 1.6 fusion.12
  132.2 2.8 fusion.16
  135.6 1.1 select_convert_fusion
  138.9 1.8 fusion.54
  140.8 27.9 %all-to-all-done.3 = bf16[64,4,6,1024]{3,1,2,0:T(4,128)(2,1)} async-done(((bf16[64,4,6,1024]{3,1,2,0:T(4,128)(2,1)}), bf16[64,4,6,1024]{3,1,2,0:T(4,128)(2,1)}, u32[]{:S(2)}, u32[]{:S(2)}) %all-to-all-start.3) | async-done | bytes 3145760 | tf_op jit(solution)/shard_map/all_to_all | solution.py:165
  168.6 5.3 copy.117
  173.9 5.4 all-to-all-start.4
  182.5 0.9 broadcast_in_dim.175
  183.5 1.9 fusion.89
  185.5 10.0 %compare_convert_fusion = f32[128]{0:T(128)S(1)} fusion(s32[]{:T(128)} %bitcast.39, s32[]{:T(128)} %bitcast.40, s32[]{:T(128)} %bitcast.41, s32[]{:T(128)} %bitcast.42, s32[]{:T(128)} %bitcast.43, s32[]{:T(128)} %bitcast.45, s32[]{:T(128)} %bitcast.44, s32[]{:T(128)} %bitcast.22, s32[]{:T(128)} %bitcast.24, s32[]{:T(128)} %bitcast.26, s32[]{:T(128)} %bitcast.28, ...), kind=kLoop, calls=%fused_computation.196 | loop fusion | flops 8064 | bytes 580 | tf_op jit(solution)/shard_map/convert_element_type | solution.py:50
  196.8 34.2 %all-reduce.8.cloned.1.call-done = f32[512,1024]{1,0:T(8,128)} async-done(((f32[512,1024]{1,0:T(8,128)}), f32[512,1024]{1,0:T(8,128)}) %all-reduce.8.cloned.1.call-update) | async-done | bytes 2097168 | tf_op jit(solution)/shard_map/psum | solution.py:133
  231.1 1.3 multiply_reduce_fusion.2
  232.3 2.0 fusion.50
  234.4 3.7 copy.118
  238.1 4.9 reshape.657
  243.0 5.3 gather_fusion.7
  248.3 2.5 fusion.2
  250.9 2.8 fusion.10
  254.0 1.7 fusion.7
  255.7 1.1 fusion.9
  257.3 1.7 fusion.6
  259.0 5.8 gather_fusion.8
  264.8 6.2 gather.58
  271.1 4.7 fusion.1
  275.8 4.2 copy.133
  279.9 5.8 all-to-all-start.5
  286.0 0.9 divide_convert_fusion.1
  286.9 28.9 %all-gather.5.cloned.1.call-done = bf16[512,1024]{1,0:T(8,128)(2,1)} async-done(((bf16[128,1024]{1,0:T(8,128)(2,1)}), bf16[512,1024]{1,0:T(8,128)(2,1)}) %all-gather.5.cloned.1.call-update) | async-done | bytes 1048592 | tf_op jit(solution)/shard_map/all_gather | solution.py:195
  315.8 1.7 fusion.26
  321.2 1.9 copy.127
  323.2 2.8 reshape.662
  326.0 6.1 convolution_bitcast_fusion
  332.2 5.2 copy.129
  337.4 21.5 %all-to-all-done.5 = bf16[64,4,6,1024]{3,1,2,0:T(4,128)(2,1)} async-done(((bf16[64,4,6,1024]{3,1,2,0:T(4,128)(2,1)}), bf16[64,4,6,1024]{3,1,2,0:T(4,128)(2,1)}, u32[]{:S(2)}, u32[]{:S(2)}) %all-to-all-start.5) | async-done | bytes 3145760 | tf_op jit(solution)/shard_map/all_to_all | solution.py:178
  358.9 5.4 copy.134
  364.3 6.6 all-to-all-start.6
  370.9 2.8 fusion.52
  375.0 163.0 %all-reduce.10.cloned.1.call-done = f32[4,1024,256]{2,0,1:T(4,128)} async-done(((f32[4,1024,256]{2,0,1:T(4,128)}), f32[4,1024,256]{2,0,1:T(4,128)}) %all-reduce.10.cloned.1.call-update) | async-done | bytes 4194320
  538.0 0.8 constant_dynamic-slice_fusion
  539.4 5.1 copy.135
  544.6 8.4 %reshape.790 = f32[1536,1024]{1,0:T(8,128)} reshape(f32[64,4,6,1024]{3,2,1,0:T(8,128)} %copy.135) | data formatting | bytes 12582912 | tf_op jit(solution)/shard_map/reshape | solution.py:193
  553.0 16.1 %scatter_custom_fusion.3 = f32[512,1024]{1,0:T(8,128)} fusion(s32[1536]{0:T(1024)} %copy-done.39, f32[1536,1024]{1,0:T(8,128)} %reshape.790, f32[]{:T(128)} %constant.182.clone.1), kind=kCustom, calls=%fused_computation.68 | custom fusion | flops 1572864 | bytes 2097664 | tf_op jit(solution)/shard_map/scatter-add | solution.py:193
  569.1 112.4 %reduce-scatter.2.cloned.1.call-done = f32[256,16]{0,1:T(8,128)} async-done(((f32[256,1024]{0,1:T(8,128)}), f32[256,16]{0,1:T(8,128)}) %reduce-scatter.2.cloned.1.call-update) | async-done | bytes 16400 | tf_op jit(solution)/shard_map/reduce_scatter | solution.py:212
  (203 shorter events, 23.9 us)
Async XLA Ops:
  7.2 125.0 %copy-start = (bf16[4,1024,256]{2,1,0:T(8,128)(2,1)S(1)}, bf16[4,1024,256]{2,1,0:T(8,128)(2,1)}, u32[]{:S(2)}) copy-start(bf16[4,1024,256]{2,1,0:T(8,128)(2,1)} %param.14) | copy-start | bytes 6291460
  8.2 0.6 copy-start.40
  9.3 5.1 copy-start.38
  9.4 0.6 copy-start.41
  14.4 6.8 copy-start.29
  14.4 6.8 copy-start.30
  15.3 19.3 %copy-start.3 = (s32[1024]{0:T(1024)S(1)}, s32[1024]{0:T(1024)}, u32[]{:S(2)}) copy-start(s32[1024]{0:T(1024)} %param.10) | copy-start | bytes 12292
  22.6 22.2 %all-to-all-start.1 = ((s32[64,4,6]{2,1,0:T(4,128)}), s32[64,4,6]{2,1,0:T(4,128)S(1)}, u32[]{:S(2)}, u32[]{:S(2)}) async-start(s32[64,4,6]{2,1,0:T(4,128)} %reshape.655), calls=%async_computation.1 | async-start | bytes 262144 | tf_op jit(solution)/shard_map/all_to_all | solution.py:156
  45.6 8.8 %all-to-all-start.2 = ((s32[4,1,384]{2,1,0:T(1,128)}), s32[4,1,384]{2,1,0:T(1,128)S(1)}, u32[]{:S(2)}, u32[]{:S(2)}) async-start(s32[4,1,384]{2,1,0:T(1,128)} %reshape.856), calls=%async_computation.2 | async-start | bytes 12288 | tf_op jit(solution)/shard_map/all_to_all | solution.py:155
  50.6 12.2 %copy-start.2 = (bf16[512,1024]{1,0:T(8,128)(2,1)S(1)}, bf16[512,1024]{1,0:T(8,128)(2,1)}, u32[]{:S(2)}) copy-start(bf16[512,1024]{1,0:T(8,128)(2,1)} %param.13) | copy-start | bytes 3145732
  54.4 34.4 %all-to-all-start = ((bf16[64,1,32,256]{3,2,1,0:T(8,128)(2,1)}), bf16[64,1,32,256]{3,2,1,0:T(8,128)(2,1)}, u32[]{:S(2)}, u32[]{:S(2)}) async-start(bf16[64,1,32,256]{3,2,1,0:T(8,128)(2,1)} %bitcast.239), calls=%async_computation | async-start | bytes 2097152 | tf_op jit(solution)/shard_map/all_to_all | solution.py:102
  62.7 5.9 copy-start.39
  88.8 79.9 %all-to-all-start.3 = ((bf16[64,4,6,1024]{3,1,2,0:T(4,128)(2,1)}), bf16[64,4,6,1024]{3,1,2,0:T(4,128)(2,1)}, u32[]{:S(2)}, u32[]{:S(2)}) async-start(bf16[64,4,6,1024]{3,1,2,0:T(4,128)(2,1)} %copy.116), calls=%async_computation.3 | async-start | bytes 6291456 | tf_op jit(solution)/shard_map/all_to_all | solution.py:165
  95.9 32.9 %all-gather.3.cloned.1.call-start = ((), (), s32[]{:S(2)}) async-start(), calls=%async_computation.8 | async-start | bytes 1310720 | tf_op jit(solution)/shard_map/all_gather | solution.py:115
  96.0 4.6 copy-start.4
  100.3 130.8 %all-reduce.8.cloned.1.call-start = ((), (), s32[]{:S(2)}) async-start(), calls=%async_computation.9 | async-start | bytes 4194304 | tf_op jit(solution)/shard_map/psum | solution.py:133
  101.2 0.5 copy-start.24
  101.2 34.4 %copy-start.47 = (f32[16]{0:T(128)}, f32[16]{0:T(128)S(1)}, u32[]{:S(2)}) copy-start(f32[16]{0:T(128)S(1)} %convert_element_type.130) | copy-start | bytes 196
  101.8 33.9 %copy-start.34 = (pred[16,32,32]{2,1,0:T(8,128)(4,1)}, pred[16,32,32]{2,1,0:T(8,128)(4,1)S(1)}, u32[]{:S(2)}) copy-start(pred[16,32,32]{2,1,0:T(8,128)(4,1)S(1)} %broadcast_and_fusion) | copy-start | bytes 49156
  128.8 3.4 copy-start.12
  130.4 4.6 copy-start.42
  132.2 2.8 copy-start.44
  135.2 1.6 copy-start.20
  135.2 1.5 copy-start.16
  135.3 1.4 copy-start.18
  135.6 2.6 copy-start.10
  136.8 4.0 copy-start.22
  136.8 2.1 copy-start.14
  137.2 1.1 copy-start.7
  137.6 0.7 copy-start.27
  138.3 2.5 copy-start.25
  173.9 60.4 %all-to-all-start.4 = ((bf16[64,4,6,1024]{3,0,2,1:T(8,128)(2,1)}), bf16[64,4,6,1024]{3,0,2,1:T(8,128)(2,1)S(1)}, u32[]{:S(2)}, u32[]{:S(2)}) async-start(bf16[64,4,6,1024]{3,0,2,1:T(8,128)(2,1)} %copy.117), calls=%async_computation.4 | async-start | bytes 6291456 | tf_op jit(solution)/shard_map/all_to_all | solution.py:164
  248.3 2.6 copy-start.5
  248.3 2.6 copy-start.33
  250.9 2.8 copy-start.36
  250.9 3.1 copy-start.9
  254.0 1.7 copy-start.37
  255.7 1.6 copy-start.6
  257.3 1.7 copy-start.31
  279.9 79.0 %all-to-all-start.5 = ((bf16[64,4,6,1024]{3,1,2,0:T(4,128)(2,1)}), bf16[64,4,6,1024]{3,1,2,0:T(4,128)(2,1)}, u32[]{:S(2)}, u32[]{:S(2)}) async-start(bf16[64,4,6,1024]{3,1,2,0:T(4,128)(2,1)} %copy.133), calls=%async_computation.6 | async-start | bytes 6291456 | tf_op jit(solution)/shard_map/all_to_all | solution.py:178
  285.7 30.1 %copy-start.15 = (bf16[256,1024]{1,0:T(8,128)(2,1)S(1)}, bf16[256,1024]{1,0:T(8,128)(2,1)}, u32[]{:S(2)}) copy-start(bf16[256,1024]{1,0:T(8,128)(2,1)} %param.15) | copy-start | bytes 1572868
  285.7 30.1 %all-gather.5.cloned.1.call-start = ((), (), s32[]{:S(2)}) async-start(), calls=%async_computation.10 | async-start | bytes 1310720 | tf_op jit(solution)/shard_map/all_gather | solution.py:195
  286.0 31.9 %copy-start.8 = (f32[16,32,2,128]{3,1,2,0:T(8,128)S(1)}, f32[16,32,2,128]{3,1,2,0:T(8,128)}, u32[]{:S(2)}) copy-start(f32[16,32,2,128]{3,1,2,0:T(8,128)} %copy-done.7) | copy-start | bytes 1572868
  286.0 31.9 %copy-start.11 = (f32[16,32,2,128]{3,2,1,0:T(2,128)S(1)}, f32[16,32,2,128]{3,2,1,0:T(2,128)}, u32[]{:S(2)}) copy-start(f32[16,32,2,128]{3,2,1,0:T(2,128)} %copy-done.10) | copy-start | bytes 1572868
  286.0 31.9 %copy-start.32 = (f32[16,32,2]{1,2,0:T(2,128)S(1)}, f32[16,32,2]{1,2,0:T(2,128)}, u32[]{:S(2)}) copy-start(f32[16,32,2]{1,2,0:T(2,128)} %get-tuple-element.29) | copy-start | bytes 12292
  286.9 31.5 %copy-start.28 = (f32[16,32,2]{1,2,0:T(2,128)S(1)}, f32[16,32,2]{1,2,0:T(2,128)}, u32[]{:S(2)}) copy-start(f32[16,32,2]{1,2,0:T(2,128)} %copy-done.27) | copy-start | bytes 12292
  286.9 31.6 %copy-start.26 = (f32[16,32,2]{1,2,0:T(2,128)S(1)}, f32[16,32,2]{1,2,0:T(2,128)}, u32[]{:S(2)}) copy-start(f32[16,32,2]{1,2,0:T(2,128)} %copy-done.25) | copy-start | bytes 12292
  286.9 251.1 %all-reduce.10.cloned.1.call-start = ((), (), s32[]{:S(2)}) async-start(), calls=%async_computation.12 | async-start | bytes 8388608
  317.8 1.3 copy-start.21
  317.8 1.3 copy-start.35
  317.8 1.3 copy-start.48
  317.8 1.3 copy-start.49
  319.2 1.0 copy-start.19
  319.2 1.2 copy-start.17
  319.2 1.4 copy-start.23
  323.2 2.9 copy-start.13
  323.2 2.9 copy-start.43
  323.2 2.9 copy-start.45
  364.3 175.2 %all-to-all-start.6 = ((bf16[64,4,6,1024]{3,0,2,1:T(8,128)(2,1)}), bf16[64,4,6,1024]{3,0,2,1:T(8,128)(2,1)S(1)}, u32[]{:S(2)}, u32[]{:S(2)}) async-start(bf16[64,4,6,1024]{3,0,2,1:T(8,128)(2,1)} %copy.134), calls=%async_computation.7 | async-start | bytes 6291456 | tf_op jit(solution)/shard_map/all_to_all | solution.py:177
  370.9 2.8 copy-start.46
  370.9 310.6 %reduce-scatter.2.cloned.1.call-start = ((), (), s32[]{:S(2)}) async-start(), calls=%async_computation.11 | async-start | bytes 1064960 | tf_op jit(solution)/shard_map/reduce_scatter | solution.py:212
  544.6 136.9 %copy-start.1 = (bf16[4,1024,256]{2,1,0:T(8,128)(2,1)S(1)}, bf16[4,1024,256]{2,1,0:T(8,128)(2,1)}, u32[]{:S(2)}) copy-start(bf16[4,1024,256]{2,1,0:T(8,128)(2,1)} %param.14) | copy-start | bytes 6291460
Sparse Core Ops, SparseCore 0:
  100.4 28.3 all-gather.2
  140.9 90.1 all-reduce.7
  288.3 27.4 all-gather.4
  337.5 200.3 all-reduce.9
  542.4 139.0 reduce-scatter.1
where the time goes:
time: 695 us; the launch traced here: 688 us
  waiting for transfers between devices  423 us (61%)
  local copies, waits for them, and re-layouts  123 us (18%)
  other arithmetic  55.8 us (8%)
  starting transfers between devices  48.5 us (7%)
  matrix products  21.9 us (3%)
  between operations  15.7 us (2%)
    unnamed x6, waiting for transfers between devices  163 us
    reduce_scatter x1, waiting for transfers between devices, per_device(): lax.psum_scatter(w_out_part, 'dp', scatter_dimension=1, tiled=True)  112 us
    psum x1, waiting for transfers between devices, per_device(): summed = lax.psum(partial_out, 'mp')  34.2 us
    all_gather x1, waiting for transfers between devices, per_device(): lax.all_gather(out_grad.astype(jnp.bfloat16), 'mp', axis=0, tiled=True)  28.9 us
    all_to_all x1, waiting for transfers between devices, per_device(): lax.all_to_all(looked, 'dp', split_axis=0, concat_axis=0, tiled=True)  27.9 us
    all_gather x1, waiting for transfers between devices, per_device(): features = lax.all_gather(local_rows, 'mp', axis=2, tiled=True)  27.1 us
    all_to_all x1, waiting for transfers between devices, per_device(): lax.all_to_all(sending.reshape(dp_count, mp_count, capacity, width).astyp...  21.5 us
    scatter-add x1, other arithmetic, per_device(): cat_grad = jnp.zeros((catalogue.shape[0], width), jnp.float32).at[incomin...  16.1 us
  transfers between devices with their start and end apart: 12, of which 9 were waited for; matrix products, arithmetic and copies ran while one was open for 20% of the time, Pallas kernels for 0%

commit v1 on v0

--- a/solution.py
+++ b/solution.py
@@ -130,7 +130,10 @@
     gated_flat = gated.reshape(rows_all, cols_heads)
     partial_out = jnp.dot(gated_flat, w_out, preferred_element_type=jnp.float32)
     quarter = rows_all // mp_count
-    summed = lax.psum(partial_out, "mp")
+    size, summed = (lax.axis_size("mp"), partial_out)
+    for hop in [1 << k for k in range(size.bit_length() - 1)]:
+        swap = [(i, i ^ hop) for i in range(size)]
+        summed = summed + lax.ppermute(summed, "mp", swap)
     out_rows = lax.dynamic_slice_in_dim(summed, here_mp * quarter, quarter, 0)
     out_rows = out_rows + lax.dynamic_slice_in_dim(flat_rows, here_mp * quarter, quarter, 0).astype(
         jnp.float32

time: 695 us -> 726 us (1.045)
  waiting for transfers between devices: 423 us -> 447 us
    ppermute x0 -> x2, waiting for transfers between devices: none -> 54 us  [per_device(): summed = summed + lax.ppermute(summed, 'mp', swap)]
    psum x1 -> x0, waiting for transfers between devices: 34.2 us -> none  [per_device(): summed = lax.psum(partial_out, 'mp')]
    all_to_all x1, waiting for transfers between devices: 0.01 us -> 28.3 us  [per_device(): lax.all_to_all(lax.all_to_all(looked, 'dp', split_axis=0, concat_axis=0,...]
    all_gather x1, waiting for transfers between devices: 27.1 us -> 0.02 us  [per_device(): features = lax.all_gather(local_rows, 'mp', axis=2, tiled=True)]
    all_to_all x1, waiting for transfers between devices: 27.9 us -> 11.1 us  [per_device(): lax.all_to_all(looked, 'dp', split_axis=0, concat_axis=0, tiled=True)]
    all_to_all x1, waiting for transfers between devices: 3.51 us -> 14.7 us  [per_device(): lax.all_to_all(outgoing, 'dp', split_axis=0, concat_axis=0, tiled=True)]
    unnamed x6 -> x5, waiting for transfers between devices: 163 us -> 162 us
  transfers between devices with their start and end apart: 12 -> 13, of which waited for: 9 -> 11; matrix products, arithmetic and copies ran while one was open for 20% -> 20% of each run, Pallas kernels for 0% -> 0%
where the time goes in v1:
time: 726 us; the launch traced here: 719 us
  waiting for transfers between devices  447 us (62%)
  local copies, waits for them, and re-layouts  120 us (17%)
  other arithmetic  60.3 us (8%)
  starting transfers between devices  54.4 us (7%)
  matrix products  21.4 us (3%)
  between operations  15.7 us (2%)
    unnamed x5, waiting for transfers between devices  162 us
    reduce_scatter x1, waiting for transfers between devices, per_device(): lax.psum_scatter(w_out_part, 'dp', scatter_dimension=1, tiled=True)  112 us
    ppermute x2, waiting for transfers between devices, per_device(): summed = summed + lax.ppermute(summed, 'mp', swap)  54 us
    all_to_all x1, waiting for transfers between devices, per_device(): lax.all_to_all(lax.all_to_all(looked, 'dp', split_axis=0, concat_axis=0,...  28.3 us
    all_gather x1, waiting for transfers between devices, per_device(): lax.all_gather(out_grad.astype(jnp.bfloat16), 'mp', axis=0, tiled=True)  26.8 us
    all_to_all x1, waiting for transfers between devices, per_device(): lax.all_to_all(sending.reshape(dp_count, mp_count, capacity, width).astyp...  24.6 us
    scatter-add x1, other arithmetic, per_device(): cat_grad = jnp.zeros((catalogue.shape[0], width), jnp.float32).at[incomin...  16.1 us
    all_to_all x1, waiting for transfers between devices, per_device(): lax.all_to_all(outgoing, 'dp', split_axis=0, concat_axis=0, tiled=True)  14.7 us
  transfers between devices with their start and end apart: 13, of which 11 were waited for; matrix products, arithmetic and copies ran while one was open for 20% of the time, Pallas kernels for 0%

profile of v1, /device:TPU:8, one launch (start us, length us, event | category | flops | bytes accessed | tf_op | source)
XLA Modules:
  0.0 719.2 jit_solution(6678038253761618875)
XLA Ops:
  8.1 1.3 gather_fusion
  9.4 4.3 scatter_custom_fusion
  15.7 2.5 scatter_fusion
  18.2 12.2 %all-to-all-start = ((bf16[64,1,32,256]{3,2,1,0:T(8,128)(2,1)}), bf16[64,1,32,256]{3,2,1,0:T(8,128)(2,1)}, u32[]{:S(2)}, u32[]{:S(2)}) async-start(bf16[64,1,32,256]{3,2,1,0:T(8,128)(2,1)} %bitcast.7), calls=%async_computation | async-start | bytes 2097152 | tf_op jit(solution)/shard_map/all_to_all | solution.py:102
  30.6 1.4 gather_fusion.2
  33.2 4.3 scatter_custom_fusion.2
  37.5 5.9 gather_fusion.5
  43.6 14.7 %all-to-all-done = bf16[64,1,32,256]{3,2,1,0:T(8,128)(2,1)} async-done(((bf16[64,1,32,256]{3,2,1,0:T(8,128)(2,1)}), bf16[64,1,32,256]{3,2,1,0:T(8,128)(2,1)}, u32[]{:S(2)}, u32[]{:S(2)}) %all-to-all-start) | async-done | bytes 1048608 | tf_op jit(solution)/shard_map/all_to_all | solution.py:102
  58.4 1.8 gather_fusion.4
  62.4 6.6 all-to-all-start.1
  69.0 10.3 %all-to-all-done.1 = s32[64,4,6]{2,1,0:T(4,128)S(1)} async-done(((s32[64,4,6]{2,1,0:T(4,128)}), s32[64,4,6]{2,1,0:T(4,128)S(1)}, u32[]{:S(2)}, u32[]{:S(2)}) %all-to-all-start.1) | async-done | bytes 6176 | tf_op jit(solution)/shard_map/all_to_all | solution.py:159
  80.0 5.1 all-to-all-start.2
  85.8 3.2 all-to-all-done.2
  90.8 5.8 gather_fusion.6
  96.6 6.2 gather.53
  102.8 2.6 broadcast_select_fusion
  105.4 7.9 %copy.116 = bf16[64,4,6,1024]{3,1,2,0:T(4,128)(2,1)} copy(bf16[64,4,6,1024]{3,2,1,0:T(8,128)(2,1)S(1)} %broadcast_select_fusion) | data formatting | bytes 6291456 | tf_op jit(solution)/shard_map/jit(_take)/select_n | solution.py:166
  113.2 5.8 all-to-all-start.3
  119.2 1.5 convert_reduce_fusion.1
  120.8 1.7 fusion.12
  122.6 2.8 fusion.16
  126.0 1.1 select_convert_fusion
  129.7 1.5 collective-permute-start
  131.2 46.1 %collective-permute-done = f32[512,1024]{1,0:T(8,128)S(1)} collective-permute-done((f32[512,1024]{1,0:T(8,128)S(1)}, f32[512,1024]{1,0:T(8,128)S(1)}, u32[]{:S(2)}, u32[]{:S(2)}) %collective-permute-start) | collective-permute-done | bytes 2097184 | tf_op jit(solution)/shard_map/ppermute | solution.py:136
  177.4 1.8 add.411
  179.2 1.5 collective-permute-start.1
  180.6 11.1 %all-to-all-done.3 = bf16[64,4,6,1024]{3,1,2,0:T(4,128)(2,1)} async-done(((bf16[64,4,6,1024]{3,1,2,0:T(4,128)(2,1)}), bf16[64,4,6,1024]{3,1,2,0:T(4,128)(2,1)}, u32[]{:S(2)}, u32[]{:S(2)}) %all-to-all-start.3) | async-done | bytes 3145760 | tf_op jit(solution)/shard_map/all_to_all | solution.py:168
  191.7 5.2 copy.117
  197.0 5.5 all-to-all-start.4
  203.2 1.5 compare_and_fusion
  209.2 10.5 %compare_convert_fusion = f32[128]{0:T(128)} fusion(s32[]{:T(128)} %bitcast.39, s32[]{:T(128)} %bitcast.40, s32[]{:T(128)} %bitcast.41, s32[]{:T(128)} %bitcast.42, s32[]{:T(128)} %bitcast.43, s32[]{:T(128)} %bitcast.45, s32[]{:T(128)} %bitcast.44, s32[]{:T(128)} %bitcast.22, s32[]{:T(128)} %bitcast.24, s32[]{:T(128)} %bitcast.26, s32[]{:T(128)} %bitcast.28, ...), kind=kLoop, calls=%fused_computation.197 | loop fusion | flops 8064 | bytes 580 | tf_op jit(solution)/shard_map/convert_element_type | solution.py:50
  220.4 1.3 compare_and_fusion.3
  221.7 7.9 %collective-permute-done.1 = f32[512,1024]{1,0:T(8,128)} collective-permute-done((f32[512,1024]{1,0:T(8,128)}, f32[512,1024]{1,0:T(8,128)}, u32[]{:S(2)}, u32[]{:S(2)}) %collective-permute-start.1) | collective-permute-done | bytes 2097184 | tf_op jit(solution)/shard_map/ppermute | solution.py:136
  229.5 1.4 multiply_reduce_fusion.2
  231.0 2.2 broadcast_divide_fusion
  233.2 28.3 %all-to-all-done.4 = bf16[64,4,6,1024]{3,0,2,1:T(8,128)(2,1)S(1)} async-done(((bf16[64,4,6,1024]{3,0,2,1:T(8,128)(2,1)}), bf16[64,4,6,1024]{3,0,2,1:T(8,128)(2,1)S(1)}, u32[]{:S(2)}, u32[]{:S(2)}) %all-to-all-start.4) | async-done | bytes 3145760 | tf_op jit(solution)/shard_map/all_to_all | solution.py:167
  261.5 3.7 copy.118
  265.2 4.9 reshape.657
  270.1 5.3 gather_fusion.7
  275.4 2.5 fusion.2
  278.1 2.8 fusion.10
  281.2 1.7 fusion.7
  283.0 1.9 fusion.9
  284.9 1.7 fusion.6
  286.6 5.8 gather_fusion.8
  292.4 6.2 gather.58
  298.6 4.4 fusion.1
  303.0 4.2 copy.133
  307.2 10.9 %all-to-all-start.5 = ((bf16[64,4,6,1024]{3,1,2,0:T(4,128)(2,1)}), bf16[64,4,6,1024]{3,1,2,0:T(4,128)(2,1)}, u32[]{:S(2)}, u32[]{:S(2)}) async-start(bf16[64,4,6,1024]{3,1,2,0:T(4,128)(2,1)} %copy.133), calls=%async_computation.6 | async-start | bytes 6291456 | tf_op jit(solution)/shard_map/all_to_all | solution.py:181
  319.4 26.8 %all-gather.5.cloned.1.call-done = bf16[512,1024]{1,0:T(8,128)(2,1)} async-done(((bf16[128,1024]{1,0:T(8,128)(2,1)}), bf16[512,1024]{1,0:T(8,128)(2,1)}) %all-gather.5.cloned.1.call-update) | async-done | bytes 1048592 | tf_op jit(solution)/shard_map/all_gather | solution.py:198
  346.2 1.7 fusion.26
  351.6 1.9 copy.127
  353.5 2.9 reshape.662
  356.4 6.1 convolution_bitcast_fusion
  362.6 5.2 copy.129
  367.8 24.6 %all-to-all-done.5 = bf16[64,4,6,1024]{3,1,2,0:T(4,128)(2,1)} async-done(((bf16[64,4,6,1024]{3,1,2,0:T(4,128)(2,1)}), bf16[64,4,6,1024]{3,1,2,0:T(4,128)(2,1)}, u32[]{:S(2)}, u32[]{:S(2)}) %all-to-all-start.5) | async-done | bytes 3145760 | tf_op jit(solution)/shard_map/all_to_all | solution.py:181
  392.4 5.3 copy.134
  397.8 5.2 all-to-all-start.6
  403.0 2.8 fusion.52
  407.1 161.9 %all-reduce.7.cloned.1.call-done = f32[4,1024,256]{2,0,1:T(4,128)} async-done(((f32[4,1024,256]{2,0,1:T(4,128)}), f32[4,1024,256]{2,0,1:T(4,128)}) %all-reduce.7.cloned.1.call-update) | async-done | bytes 4194320
  570.5 5.2 copy.135
  575.6 8.4 %reshape.790 = f32[1536,1024]{1,0:T(8,128)} reshape(f32[64,4,6,1024]{3,2,1,0:T(8,128)} %copy.135) | data formatting | bytes 12582912 | tf_op jit(solution)/shard_map/reshape | solution.py:196
  584.1 16.1 %scatter_custom_fusion.3 = f32[512,1024]{1,0:T(8,128)} fusion(s32[1536]{0:T(1024)S(1)} %fusion.73, f32[1536,1024]{1,0:T(8,128)} %reshape.790, f32[]{:T(128)} %constant.182.clone.1), kind=kCustom, calls=%fused_computation.68 | custom fusion | flops 1572864 | bytes 2097664 | tf_op jit(solution)/shard_map/scatter-add | solution.py:196
  600.1 112.3 %reduce-scatter.2.cloned.1.call-done = f32[256,16]{0,1:T(8,128)} async-done(((f32[256,1024]{0,1:T(8,128)}), f32[256,16]{0,1:T(8,128)}) %reduce-scatter.2.cloned.1.call-update) | async-done | bytes 16400 | tf_op jit(solution)/shard_map/reduce_scatter | solution.py:215
  (207 shorter events, 26.5 us)
Async XLA Ops:
  7.2 115.4 %copy-start = (bf16[4,1024,256]{2,1,0:T(8,128)(2,1)S(1)}, bf16[4,1024,256]{2,1,0:T(8,128)(2,1)}, u32[]{:S(2)}) copy-start(bf16[4,1024,256]{2,1,0:T(8,128)(2,1)} %param.14) | copy-start | bytes 6291460
  7.2 8.5 %copy-start.23 = (bf16[16,32,256]{2,1,0:T(8,128)(2,1)S(1)}, bf16[16,32,256]{2,1,0:T(8,128)(2,1)}, u32[]{:S(2)}) copy-start(bf16[16,32,256]{2,1,0:T(8,128)(2,1)} %param.8) | copy-start | bytes 786436
  18.2 40.2 %all-to-all-start = ((bf16[64,1,32,256]{3,2,1,0:T(8,128)(2,1)}), bf16[64,1,32,256]{3,2,1,0:T(8,128)(2,1)}, u32[]{:S(2)}, u32[]{:S(2)}) async-start(bf16[64,1,32,256]{3,2,1,0:T(8,128)(2,1)} %bitcast.7), calls=%async_computation | async-start | bytes 2097152 | tf_op jit(solution)/shard_map/all_to_all | solution.py:102
  30.4 88.8 %all-gather.3.cloned.1.call-start = ((), (), s32[]{:S(2)}) async-start(), calls=%async_computation.8 | async-start | bytes 1310720 | tf_op jit(solution)/shard_map/all_gather | solution.py:115
  30.6 1.5 copy-start.37
  30.6 1.8 copy-start.38
  32.3 0.9 copy-start.32
  33.1 4.4 copy-start.33
  43.4 41.7 %copy-start.3 = (s32[1024]{0:T(1024)S(1)}, s32[1024]{0:T(1024)}, u32[]{:S(2)}) copy-start(s32[1024]{0:T(1024)} %param.9) | copy-start | bytes 12292
  43.4 47.4 %copy-start.2 = (bf16[512,1024]{1,0:T(8,128)(2,1)S(1)}, bf16[512,1024]{1,0:T(8,128)(2,1)}, u32[]{:S(2)}) copy-start(bf16[512,1024]{1,0:T(8,128)(2,1)} %param.13) | copy-start | bytes 3145732
  62.4 16.9 %all-to-all-start.1 = ((s32[64,4,6]{2,1,0:T(4,128)}), s32[64,4,6]{2,1,0:T(4,128)S(1)}, u32[]{:S(2)}, u32[]{:S(2)}) async-start(s32[64,4,6]{2,1,0:T(4,128)} %reshape.655), calls=%async_computation.1 | async-start | bytes 262144 | tf_op jit(solution)/shard_map/all_to_all | solution.py:159
  80.0 8.9 %all-to-all-start.2 = ((s32[4,1,384]{2,1,0:T(1,128)}), s32[4,1,384]{2,1,0:T(1,128)S(1)}, u32[]{:S(2)}, u32[]{:S(2)}) async-start(s32[4,1,384]{2,1,0:T(1,128)} %reshape.856), calls=%async_computation.2 | async-start | bytes 12288 | tf_op jit(solution)/shard_map/all_to_all | solution.py:158
  85.8 40.2 %copy-start.48 = (f32[16]{0:T(128)}, f32[16]{0:T(128)S(1)}, u32[]{:S(2)}) copy-start(f32[16]{0:T(128)S(1)} %convert_element_type.130) | copy-start | bytes 196
  113.2 78.5 %all-to-all-start.3 = ((bf16[64,4,6,1024]{3,1,2,0:T(4,128)(2,1)}), bf16[64,4,6,1024]{3,1,2,0:T(4,128)(2,1)}, u32[]{:S(2)}, u32[]{:S(2)}) async-start(bf16[64,4,6,1024]{3,1,2,0:T(4,128)(2,1)} %copy.116), calls=%async_computation.3 | async-start | bytes 6291456 | tf_op jit(solution)/shard_map/all_to_all | solution.py:168
  119.1 6.8 copy-start.26
  119.2 3.4 copy-start.11
  120.8 4.6 copy-start.42
  122.5 2.8 copy-start.44
  125.5 1.6 copy-start.19
  125.6 1.5 copy-start.15
  125.7 1.4 copy-start.17
  126.0 2.6 copy-start.9
  127.1 2.5 copy-start.21
  127.1 2.1 copy-start.13
  127.5 2.2 copy-start.7
  129.7 47.7 %collective-permute-start = (f32[512,1024]{1,0:T(8,128)S(1)}, f32[512,1024]{1,0:T(8,128)S(1)}, u32[]{:S(2)}, u32[]{:S(2)}) collective-permute-start(f32[512,1024]{1,0:T(8,128)S(1)} %fusion.54), channel_id=1, source_target_pairs={{0,1},{1,0},{2,3},{3,2},{4,5},{5,4},{6,7},{7,6},{8,9},{9,8},{10,11... | collective-permute-start | bytes 6291464 | tf_op jit(solution)/shard_map/ppermute | solution.py:136
  179.2 50.4 %collective-permute-start.1 = (f32[512,1024]{1,0:T(8,128)}, f32[512,1024]{1,0:T(8,128)}, u32[]{:S(2)}, u32[]{:S(2)}) collective-permute-start(f32[512,1024]{1,0:T(8,128)} %add.411), channel_id=1, source_target_pairs={{0,2},{1,3},{2,0},{3,1},{4,6},{5,7},{6,4},{7,5},{8,10},{9,11},{10,... | collective-permute-start | bytes 6291464 | tf_op jit(solution)/shard_map/ppermute | solution.py:136
  197.0 64.5 %all-to-all-start.4 = ((bf16[64,4,6,1024]{3,0,2,1:T(8,128)(2,1)}), bf16[64,4,6,1024]{3,0,2,1:T(8,128)(2,1)S(1)}, u32[]{:S(2)}, u32[]{:S(2)}) async-start(bf16[64,4,6,1024]{3,0,2,1:T(8,128)(2,1)} %copy.117), calls=%async_computation.4 | async-start | bytes 6291456 | tf_op jit(solution)/shard_map/all_to_all | solution.py:167
  205.5 69.9 %copy-start.34 = (pred[1024]{0:T(1024)(128)(4,1)}, pred[1024]{0:T(1024)(128)(4,1)S(1)}, u32[]{:S(2)}) copy-start(pred[1024]{0:T(1024)(128)(4,1)S(1)} %broadcast_in_dim.164) | copy-start | bytes 3076
  231.0 34.2 %copy-start.39 = (f32[128]{0:T(128)}, f32[128]{0:T(128)S(1)}, u32[]{:S(2)}) copy-start(f32[128]{0:T(128)S(1)} %add_sqrt_fusion.2) | copy-start | bytes 1540
  275.4 2.6 copy-start.4
  275.4 2.6 copy-start.25
  278.0 2.8 copy-start.28
  278.1 2.9 copy-start.41
  278.1 2.9 copy-start.46
  278.1 3.1 copy-start.6
  278.1 3.1 copy-start.35
  281.2 1.7 copy-start.29
  282.9 1.9 copy-start.5
  283.0 1.9 copy-start.36
  292.4 6.2 copy-start.30
  292.4 6.2 copy-start.31
  307.2 11.2 %copy-start.40 = (f32[128]{0:T(128)S(1)}, f32[128]{0:T(128)}, u32[]{:S(2)}) copy-start(f32[128]{0:T(128)} %copy-done.39) | copy-start | bytes 1540
  307.2 85.2 %all-to-all-start.5 = ((bf16[64,4,6,1024]{3,1,2,0:T(4,128)(2,1)}), bf16[64,4,6,1024]{3,1,2,0:T(4,128)(2,1)}, u32[]{:S(2)}, u32[]{:S(2)}) async-start(bf16[64,4,6,1024]{3,1,2,0:T(4,128)(2,1)} %copy.133), calls=%async_computation.6 | async-start | bytes 6291456 | tf_op jit(solution)/shard_map/all_to_all | solution.py:181
  318.1 28.0 %copy-start.14 = (bf16[256,1024]{1,0:T(8,128)(2,1)S(1)}, bf16[256,1024]{1,0:T(8,128)(2,1)}, u32[]{:S(2)}) copy-start(bf16[256,1024]{1,0:T(8,128)(2,1)} %param.15) | copy-start | bytes 1572868
  318.1 28.0 %all-gather.5.cloned.1.call-start = ((), (), s32[]{:S(2)}) async-start(), calls=%async_computation.9 | async-start | bytes 1310720 | tf_op jit(solution)/shard_map/all_gather | solution.py:198
  318.4 29.8 %copy-start.8 = (f32[16,32,2,128]{3,1,2,0:T(8,128)S(1)}, f32[16,32,2,128]{3,1,2,0:T(8,128)}, u32[]{:S(2)}) copy-start(f32[16,32,2,128]{3,1,2,0:T(8,128)} %copy-done.7) | copy-start | bytes 1572868
  318.4 29.8 %copy-start.10 = (f32[16,32,2,128]{3,2,1,0:T(2,128)S(1)}, f32[16,32,2,128]{3,2,1,0:T(2,128)}, u32[]{:S(2)}) copy-start(f32[16,32,2,128]{3,2,1,0:T(2,128)} %copy-done.9) | copy-start | bytes 1572868
  318.4 29.8 %copy-start.24 = (f32[16,32,2]{1,2,0:T(2,128)S(1)}, f32[16,32,2]{1,2,0:T(2,128)}, u32[]{:S(2)}) copy-start(f32[16,32,2]{1,2,0:T(2,128)} %get-tuple-element.29) | copy-start | bytes 12292
  319.3 249.7 %all-reduce.7.cloned.1.call-start = ((), (), s32[]{:S(2)}) async-start(), calls=%async_computation.11 | async-start | bytes 8388608
  348.1 1.3 copy-start.20
  348.2 1.3 copy-start.27
  348.2 1.3 copy-start.49
  348.2 1.3 copy-start.50
  349.5 1.0 copy-start.18
  349.5 1.2 copy-start.16
  349.5 1.4 copy-start.22
  353.5 2.9 copy-start.12
  353.5 2.9 copy-start.43
  353.5 2.9 copy-start.45
  397.8 172.7 %all-to-all-start.6 = ((bf16[64,4,6,1024]{3,0,2,1:T(8,128)(2,1)}), bf16[64,4,6,1024]{3,0,2,1:T(8,128)(2,1)S(1)}, u32[]{:S(2)}, u32[]{:S(2)}) async-start(bf16[64,4,6,1024]{3,0,2,1:T(8,128)(2,1)} %copy.134), calls=%async_computation.7 | async-start | bytes 6291456 | tf_op jit(solution)/shard_map/all_to_all | solution.py:180
  403.0 2.9 copy-start.47
  403.0 309.5 %reduce-scatter.2.cloned.1.call-start = ((), (), s32[]{:S(2)}) async-start(), calls=%async_computation.10 | async-start | bytes 1064960 | tf_op jit(solution)/shard_map/reduce_scatter | solution.py:215
  575.6 136.8 %copy-start.1 = (bf16[4,1024,256]{2,1,0:T(8,128)(2,1)S(1)}, bf16[4,1024,256]{2,1,0:T(8,128)(2,1)}, u32[]{:S(2)}) copy-start(bf16[4,1024,256]{2,1,0:T(8,128)(2,1)} %param.14) | copy-start | bytes 6291460
Sparse Core Ops, SparseCore 0:
  61.1 24.8 all-gather.2
  320.8 25.3 all-gather.4
  368.0 200.9 all-reduce.6
  573.4 139.0 reduce-scatter.1
